TPU v7x, 32 devices: a whole 2x2x4 slice. The times are simulated.
32 devices in a mesh: layer: 2 (over core), latent: 8 (over z, x), token: 2 (over y).
Axes of the slice: x: 2, y: 2, z: 4, core: 2. Of those that a mesh axis runs over, the one named last changes fastest.
Arguments:
- taps: bfloat16 [2, 448, 3584], P('layer', 'token'), may hold values from -6 to 6
- token_ids: int32 [448], P('token'), may hold values from 2 to 255999, as said below
- enc_weight: bfloat16 [2, 3584, 2048], P('layer', 'token', 'latent'), may hold values from -0.0625 to 0.0625
- enc_bias: float32 [2048], P('latent'), may hold values from -3 to 3
- dec_weight: bfloat16 [2, 3584, 2048], P('layer', 'token', 'latent'), as said below
- dec_bias: float32 [2, 3584], P('layer'), may hold values from -3 to 3
Outputs:
- enc_grad: bfloat16 [2, 3584, 2048], P('layer', 'token', 'latent')
- dec_grad: bfloat16 [2, 3584, 2048], P('layer', 'token', 'latent')
Inputs may be any that keep to these rules, and one draw needn't show every extreme that they name: `token_ids`: id 2 marks the beginning of a document and stands at position 0; all other ids are 3 or more. `dec_weight`: entries of order 2048^-0.5.
All inputs are finite; a program needn't handle non-finite values.
Results may differ from a plain program's by a relative error of at most 0.014.
Values may be sent and summed in bfloat16 or wider, within the bound.
No kernel may reach another device: no remote copies, remote signals or barrier semaphores. Data moves between devices by JAX's collectives and lax.ppermute only.
A program may use at most 64 MiB of HBM per device.

v0:
```python
import math
import jax
import jax.numpy as jnp
from jax import lax
from jax.sharding import PartitionSpec as P

KNEE_WIDTH = 0.5
SPARSITY = 0.5
BEGIN_TOKEN = 2


def smooth_relu(preact):
    positive = jnp.maximum(preact, 0.0)
    return jnp.where(
        positive < KNEE_WIDTH, positive * positive / (2.0 * KNEE_WIDTH), positive - 0.5 * KNEE_WIDTH
    )


def relu_slope(preact):
    return jnp.clip(preact / KNEE_WIDTH, 0.0, 1.0)


def local(taps, token_ids, enc_weight, enc_bias, dec_weight, dec_bias):
    tap_rows = taps[0]
    tokens_dev = tap_rows.shape[0]
    latent_dev = enc_weight.shape[2]
    row_block = enc_weight.shape[1]
    loss_scale = 1.0 / math.sqrt(tokens_dev * lax.axis_size("token"))
    keep_mask = (token_ids != BEGIN_TOKEN).astype(jnp.float32)
    spread = lax.all_to_all(tap_rows, "token", split_axis=1, concat_axis=0, tiled=True)
    partial_pre = lax.psum_scatter(
        jnp.dot(spread, enc_weight[0], preferred_element_type=jnp.float32),
        "token",
        scatter_dimension=0,
        tiled=True,
    )
    preact = lax.psum(partial_pre, "layer") + enc_bias[None, :]
    features = smooth_relu(preact).astype(jnp.bfloat16)
    dec_full = lax.all_gather(dec_weight[0], "token", axis=0, tiled=True)
    rebuilt_part = lax.dot_general(
        features, dec_full, (((1,), (1,)), ((), ())), preferred_element_type=jnp.float32
    )
    rebuilt = lax.psum(rebuilt_part, "latent") + dec_bias[0][None, :]
    residue = (loss_scale * keep_mask[:, None] * (rebuilt - tap_rows.astype(jnp.float32))).astype(
        jnp.bfloat16
    )
    colnorm = jnp.sqrt(jnp.sum(jnp.square(dec_full.astype(jnp.float32)), axis=0) + 1e-06)
    back_part = jnp.dot(residue, dec_full, preferred_element_type=jnp.float32)
    feat_back, norm_total = lax.psum((back_part, colnorm), "layer")
    feat_grads = feat_back + loss_scale * SPARSITY * keep_mask[:, None] * norm_total[None, :]
    pre_grads = (feat_grads * relu_slope(preact)).astype(jnp.bfloat16)
    activity = jnp.sum(keep_mask[:, None] * features.astype(jnp.float32), axis=0)
    penalty_scale = loss_scale * SPARSITY * activity / colnorm
    product = lax.dot_general(
        residue, features, (((0,), (0,)), ((), ())), preferred_element_type=jnp.float32
    )
    dec_grad = lax.psum_scatter(
        (product + dec_full.astype(jnp.float32) * penalty_scale[None, :]).astype(jnp.bfloat16),
        "token",
        scatter_dimension=0,
        tiled=True,
    )
    code_rows = lax.all_gather(pre_grads, "token", axis=0, tiled=True)
    blocks = lax.axis_size("token")
    spread_blocks = spread.reshape(blocks, tokens_dev, row_block)
    code_blocks = code_rows.reshape(blocks, tokens_dev, latent_dev)
    block_terms = jnp.einsum(
        "btd,btk->bdk", spread_blocks, code_blocks, preferred_element_type=jnp.float32
    )
    enc_grad = jnp.sum(
        lax.optimization_barrier(block_terms.astype(jnp.bfloat16)).astype(jnp.float32), axis=0
    )
    return (enc_grad.astype(jnp.bfloat16)[None], dec_grad[None])


def solution(mesh):
    placed = (
        P("layer", "token", None),
        P("token"),
        P("layer", "token", "latent"),
        P("latent"),
        P("layer", "token", "latent"),
        P("layer", None),
    )
    return jax.shard_map(
        local,
        mesh=mesh,
        in_specs=placed,
        out_specs=(P("layer", "token", "latent"), P("layer", "token", "latent")),
        check_vma=False,
    )
```

profile of v0, /device:TPU:0, one launch (start us, length us, event | category | flops | bytes accessed | tf_op | source)
XLA Modules:
  0.0 302.7 jit_solution(5209254433351047432)
XLA Ops:
  7.2 0.0 copy-start
  7.2 0.0 reduce-scatter.3.cloned.1.call-start
  7.2 3.7 %all_to_all.14 = bf16[224,2,1792]{2,1,0:T(2,128)(2,1)S(1)} reshape(bf16[1,224,3584]{2,1,0:T(8,128)(2,1)} %param.6) | data formatting | bytes 3211264 | tf_op jit(solution)/shard_map/all_to_all | solution.py:30
  10.9 0.2 copy.9
  11.1 23.6 %all_to_all.19 = bf16[224,2,1792]{2,0,1:T(8,128)(2,1)S(1)} all-to-all(bf16[224,2,1792]{2,0,1:T(8,128)(2,1)S(1)} %copy.9), channel_id=1, replica_groups=mesh['layer'=2,'latent'=8,'token'=2] {'token'}, dimensions={1} | all-to-all | bytes 3211264 | tf_op jit(solution)/shard_map/all_to_all | solution.py:30
  34.7 0.0 copy-start.3
  34.7 1.3 copy-done.3
  36.0 0.0 copy-done
  36.0 0.0 copy-start.7
  36.0 0.0 copy-start.6
  36.0 1.4 fusion.10
  37.4 0.0 reduce-scatter.3.cloned.1.call-update
  37.4 0.0 all-reduce.4.cloned.1.call-start
  37.4 14.5 %reduce-scatter.3.cloned.1.call-done = f32[224,256]{1,0:T(8,128)} async-done(((f32[448,256]{1,0:T(8,128)}), f32[224,256]{1,0:T(8,128)}) %reduce-scatter.3.cloned.1.call-update) | async-done | bytes 229392 | tf_op jit(solution)/shard_map/reduce_scatter | solution.py:31
  51.9 0.0 all-reduce.4.cloned.1.call-update
  52.0 0.0 all-gather.3.cloned.1.call-start
  52.0 0.7 all-gather.3.cloned.1.call-update
  52.7 0.0 all-reduce.6.cloned.1.call-start
  52.8 0.0 copy-done.7
  52.8 19.7 %all-reduce.4.cloned.1.call-done = f32[224,256]{1,0:T(8,128)} async-done(((f32[224,256]{1,0:T(8,128)}), f32[224,256]{1,0:T(8,128)}) %all-reduce.4.cloned.1.call-update) | async-done | bytes 229392 | tf_op jit(solution)/shard_map/psum | solution.py:37
  72.4 0.0 copy-done.6
  72.4 1.1 multiply_reduce_fusion
  73.5 31.9 %all-gather.3.cloned.1.call-done = bf16[1,3584,256]{2,1,0:T(8,128)(2,1)} async-done(((bf16[1,1792,256]{2,1,0:T(8,128)(2,1)}), bf16[1,3584,256]{2,1,0:T(8,128)(2,1)}) %all-gather.3.cloned.1.call-update) | async-done | bytes 1835024 | tf_op jit(solution)/shard_map/all_gather | solution.py:39
  105.4 3.9 %fusion.7 = f32[224,3584]{1,0:T(8,128)} fusion(bf16[224,256]{1,0:T(8,128)(2,1)S(1)} %get-tuple-element.5, bf16[1,3584,256]{2,1,0:T(8,128)(2,1)} %all-gather.3.cloned.1.call-done), kind=kOutput, calls=%fused_computation.12 | convolution fusion | flops 411041792 | bytes 5160960 | tf_op jit(solution)/shard_map/dot_general | solution.py:40
  109.3 0.0 copy-start.5
  109.3 0.0 copy-start.1
  109.3 0.0 all-reduce.6.cloned.1.call-update
  109.3 0.0 all-reduce.8.cloned.1.call-start
  109.4 0.6 copy-done.5
  110.1 0.8 copy-done.1
  110.8 0.5 fusion.1
  111.3 129.0 %all-reduce.6.cloned.1.call-done = f32[224,3584]{1,0:T(8,128)} async-done(((f32[224,3584]{1,0:T(8,128)}), f32[224,3584]{1,0:T(8,128)}) %all-reduce.6.cloned.1.call-update) | async-done | bytes 3211280 | tf_op jit(solution)/shard_map/psum | solution.py:43
  240.3 2.9 fusion.3
  243.2 0.0 copy-start.2
  243.2 1.1 copy-done.2
  244.3 1.3 fusion.5
  245.6 0.0 all-reduce.8.cloned.1.call-update
  245.6 0.0 reduce-scatter.5.cloned.1.call-start
  245.7 3.4 %fusion = bf16[3584,256]{1,0:T(8,128)(2,1)} fusion(bf16[224,3584]{1,0:T(8,128)(2,1)} %copy-done.2, bf16[224,256]{1,0:T(8,128)(2,1)S(1)} %get-tuple-element.5, bf16[1,3584,256]{2,1,0:T(8,128)(2,1)S(1)} %copy-done.1, f32[256]{0:T(256)S(1)} %get-tuple-element.6), kind=kOutput, calls=%fused_computation.1 | convolution fusion | flops 414711808 | bytes 5391360 | tf_op jit(solution)/shard_map/dot_general | solution.py:54
  249.1 0.0 copy-start.4
  249.1 0.0 reduce-scatter.5.cloned.1.call-update
  249.1 2.6 psum.31
  251.7 11.2 %all-reduce.8.cloned.1.call-done = f32[224,256]{1,0:T(8,128)} async-done(((f32[224,256]{1,0:T(8,128)}), f32[224,256]{1,0:T(8,128)}) %all-reduce.8.cloned.1.call-update) | async-done | bytes 229392 | tf_op jit(solution)/shard_map/psum | solution.py:49
  262.9 0.0 copy-done.4
  262.9 1.0 multiply_convert_fusion
  264.0 6.0 %all_gather.7 = bf16[448,256]{1,0:T(8,128)(2,1)S(1)} all-gather(bf16[224,256]{1,0:T(8,128)(2,1)S(1)} %multiply_convert_fusion), channel_id=1, replica_groups=mesh['layer'=2,'latent'=8,'token'=2] {'token'}, dimensions={0}, use_global_device_ids=true | all-gather | bytes 344064 | tf_op jit(solution)/shard_map/all_gather | solution.py:63
  270.0 2.1 fusion.4
  272.1 1.5 reduce_sum.31
  273.6 2.2 copy.10
  275.8 20.1 %reduce-scatter.5.cloned.1.call-done = bf16[1792,256]{1,0:T(8,128)(2,1)} async-done(((bf16[3584,256]{1,0:T(8,128)(2,1)}), bf16[1792,256]{1,0:T(8,128)(2,1)}) %reduce-scatter.5.cloned.1.call-update) | async-done | bytes 917520 | tf_op jit(solution)/shard_map/reduce_scatter | solution.py:57
  (4 shorter events, 0.1 us)
Async XLA Ops:
  7.2 28.9 %copy-start = (bf16[1,1792,256]{2,1,0:T(8,128)(2,1)S(1)}, bf16[1,1792,256]{2,1,0:T(8,128)(2,1)}, u32[]{:S(2)}) copy-start(bf16[1,1792,256]{2,1,0:T(8,128)(2,1)} %param.8) | copy-start | bytes 2752516
  7.2 44.8 %reduce-scatter.3.cloned.1.call-start = ((), (), s32[]{:S(2)}) async-start(), calls=%async_computation.3 | async-start | bytes 688128 | tf_op jit(solution)/shard_map/reduce_scatter | solution.py:31
  34.7 1.3 copy-start.3
  36.0 16.7 %copy-start.7 = (s32[224]{0:T(256)S(1)}, s32[224]{0:T(256)}, u32[]{:S(2)}) copy-start(s32[224]{0:T(256)} %param.7) | copy-start | bytes 2692
  36.0 36.4 %copy-start.6 = (f32[256]{0:T(256)S(1)}, f32[256]{0:T(256)}, u32[]{:S(2)}) copy-start(f32[256]{0:T(256)} %param.9) | copy-start | bytes 3076
  37.4 35.0 %all-reduce.4.cloned.1.call-start = ((), (), s32[]{:S(2)}) async-start(), calls=%async_computation.4 | async-start | bytes 458752 | tf_op jit(solution)/shard_map/psum | solution.py:37
  52.0 53.4 %all-gather.3.cloned.1.call-start = ((), (), s32[]{:S(2)}) async-start(), calls=%async_computation.8 | async-start | bytes 2752512 | tf_op jit(solution)/shard_map/all_gather | solution.py:39
  52.7 187.6 %all-reduce.6.cloned.1.call-start = ((), (), s32[]{:S(2)}) async-start(), calls=%async_computation.5 | async-start | bytes 6422528 | tf_op jit(solution)/shard_map/psum | solution.py:43
  109.3 0.7 copy-start.5
  109.3 1.5 copy-start.1
  109.3 153.6 %all-reduce.8.cloned.1.call-start = ((), (), s32[]{:S(2)}) async-start(), calls=%async_computation.6 | async-start | bytes 458752 | tf_op jit(solution)/shard_map/psum | solution.py:49
  243.2 1.2 copy-start.2
  245.6 50.3 %reduce-scatter.5.cloned.1.call-start = ((), (), s32[]{:S(2)}) async-start(), calls=%async_computation.7 | async-start | bytes 2752512 | tf_op jit(solution)/shard_map/reduce_scatter | solution.py:57
  249.1 13.9 %copy-start.4 = (f32[224,256]{1,0:T(8,128)S(1)}, f32[224,256]{1,0:T(8,128)}, u32[]{:S(2)}) copy-start(f32[224,256]{1,0:T(8,128)} %all-reduce.4.cloned.1.call-done) | copy-start | bytes 688132
Sparse Core Ops, SparseCore 0:
  37.5 14.3 reduce-scatter.2
  54.3 18.1 all-reduce.3
  74.0 31.3 all-gather.2
  109.5 130.8 all-reduce.5
  245.8 17.1 all-reduce.7
  265.6 30.2 reduce-scatter.4
where the time goes:
time: 303 us
  waiting for transfers between devices  227 us (75%)
  blocking collectives  32.2 us (11%)
  between operations  14.2 us (5%)
  matrix products  12 us (4%)
  local copies, waits for them, and re-layouts  9.91 us (3%)
  other arithmetic  7.02 us (2%)
    psum x1, waiting for transfers between devices, local(): rebuilt = lax.psum(rebuilt_part, 'latent') + dec_bias[0][None, :]  129 us
    all_gather x1, waiting for transfers between devices, local(): dec_full = lax.all_gather(dec_weight[0], 'token', axis=0, tiled=True)  31.9 us
    all_to_all x1, blocking collectives, local(): lax.all_to_all(tap_rows, 'token', split_axis=1, concat_axis=0, tiled=True)  23.6 us
    reduce_scatter x1, waiting for transfers between devices, local(): lax.psum_scatter((product + dec_full.astype(jnp.float32) * penalty_scale[...  20.1 us
    psum x1, waiting for transfers between devices, local(): preact = lax.psum(partial_pre, 'layer') + enc_bias[None, :]  19.7 us
    reduce_scatter x1, waiting for transfers between devices, local(): lax.psum_scatter(jnp.dot(spread, enc_weight[0], preferred_element_type=jn...  14.5 us
    psum x1, waiting for transfers between devices, local(): feat_back, norm_total = lax.psum((back_part, colnorm), 'layer')  11.2 us
  transfers between devices with their start and end apart: 6, of which 6 were waited for; matrix products, arithmetic and copies ran while one was open for 4% of the time, Pallas kernels for 0%

commit v1 on v0

--- a/solution.py
+++ b/solution.py
@@ -7,6 +7,12 @@
 KNEE_WIDTH = 0.5
 SPARSITY = 0.5
 BEGIN_TOKEN = 2
+
+
+def divide_the_islands(here_x, which_axis):
+    o_now = jax.lax.all_gather(here_x, which_axis)
+    new = jnp.sum(o_now, axis=0)
+    return new
 
 
 def smooth_relu(preact):
@@ -40,7 +46,7 @@
     rebuilt_part = lax.dot_general(
         features, dec_full, (((1,), (1,)), ((), ())), preferred_element_type=jnp.float32
     )
-    rebuilt = lax.psum(rebuilt_part, "latent") + dec_bias[0][None, :]
+    rebuilt = divide_the_islands(rebuilt_part, "latent") + dec_bias[0][None, :]
     residue = (loss_scale * keep_mask[:, None] * (rebuilt - tap_rows.astype(jnp.float32))).astype(
         jnp.bfloat16
     )

time: 303 us -> 675 us (2.23)
  waiting for transfers between devices: 227 us -> 587 us
  other arithmetic: 7.02 us -> 18.6 us
    all_gather x0 -> x1, waiting for transfers between devices: none -> 488 us  [divide_the_islands(): o_now = jax.lax.all_gather(here_x, which_axis)]
    psum x1 -> x0, waiting for transfers between devices: 129 us -> none  [local(): rebuilt = lax.psum(rebuilt_part, 'latent') + dec_bias[0][None, :]]
    reduce_sum x0 -> x1, other arithmetic: none -> 11.5 us  [divide_the_islands(): new = jnp.sum(o_now, axis=0)]
  transfers between devices with their start and end apart: 6 -> 6, of which waited for: 6 -> 6; matrix products, arithmetic and copies ran while one was open for 4% -> 2% of each run, Pallas kernels for 0% -> 0%
where the time goes in v1:
time: 675 us; the launch traced here: 674 us
  waiting for transfers between devices  587 us (87%)
  blocking collectives  32.2 us (5%)
  other arithmetic  18.6 us (3%)
  between operations  14.2 us (2%)
  matrix products  12 us (2%)
  local copies, waits for them, and re-layouts  9.8 us (1%)
    all_gather x1, waiting for transfers between devices, divide_the_islands(): o_now = jax.lax.all_gather(here_x, which_axis)  488 us
    all_gather x1, waiting for transfers between devices, local(): dec_full = lax.all_gather(dec_weight[0], 'token', axis=0, tiled=True)  31.9 us
    all_to_all x1, blocking collectives, local(): lax.all_to_all(tap_rows, 'token', split_axis=1, concat_axis=0, tiled=True)  23.6 us
    reduce_scatter x1, waiting for transfers between devices, local(): lax.psum_scatter((product + dec_full.astype(jnp.float32) * penalty_scale[...  20.1 us
    psum x1, waiting for transfers between devices, local(): preact = lax.psum(partial_pre, 'layer') + enc_bias[None, :]  19.7 us
    reduce_scatter x1, waiting for transfers between devices, local(): lax.psum_scatter(jnp.dot(spread, enc_weight[0], preferred_element_type=jn...  14.5 us
  transfers between devices with their start and end apart: 6, of which 6 were waited for; matrix products, arithmetic and copies ran while one was open for 2% of the time, Pallas kernels for 0%

profile of v1, /device:TPU:0, one launch (start us, length us, event | category | flops | bytes accessed | tf_op | source)
XLA Modules:
  0.0 674.5 jit_solution(6176081308186872619)
XLA Ops:
  7.2 0.0 copy-start
  7.2 0.0 reduce-scatter.3.cloned.1.call-start
  7.2 3.7 all_to_all.14
  10.9 0.2 copy.9
  11.1 23.6 %all_to_all.19 = bf16[224,2,1792]{2,0,1:T(8,128)(2,1)S(1)} all-to-all(bf16[224,2,1792]{2,0,1:T(8,128)(2,1)S(1)} %copy.9), channel_id=1, replica_groups=mesh['layer'=2,'latent'=8,'token'=2] {'token'}, dimensions={1} | all-to-all | bytes 3211264 | tf_op jit(solution)/shard_map/all_to_all | solution.py:36
  34.7 0.0 copy-start.3
  34.7 1.2 copy-done.3
  35.9 0.0 copy-done
  35.9 0.0 copy-start.7
  35.9 0.0 copy-start.6
  35.9 1.4 fusion.10
  37.3 0.0 reduce-scatter.3.cloned.1.call-update
  37.3 0.0 all-reduce.3.cloned.1.call-start
  37.3 14.5 %reduce-scatter.3.cloned.1.call-done = f32[224,256]{1,0:T(8,128)} async-done(((f32[448,256]{1,0:T(8,128)}), f32[224,256]{1,0:T(8,128)}) %reduce-scatter.3.cloned.1.call-update) | async-done | bytes 229392 | tf_op jit(solution)/shard_map/reduce_scatter | solution.py:37
  51.8 0.0 all-reduce.3.cloned.1.call-update
  51.9 0.0 all-gather.5.cloned.1.call-start
  51.9 0.7 all-gather.5.cloned.1.call-update
  52.6 0.0 all-gather.7.cloned.1.call-start
  52.6 0.0 copy-done.7
  52.7 19.7 %all-reduce.3.cloned.1.call-done = f32[224,256]{1,0:T(8,128)} async-done(((f32[224,256]{1,0:T(8,128)}), f32[224,256]{1,0:T(8,128)}) %all-reduce.3.cloned.1.call-update) | async-done | bytes 229392 | tf_op jit(solution)/shard_map/psum | solution.py:43
  72.3 0.0 copy-done.6
  72.3 1.1 multiply_reduce_fusion
  73.4 31.9 %all-gather.5.cloned.1.call-done = bf16[1,3584,256]{2,1,0:T(8,128)(2,1)} async-done(((bf16[1,1792,256]{2,1,0:T(8,128)(2,1)}), bf16[1,3584,256]{2,1,0:T(8,128)(2,1)}) %all-gather.5.cloned.1.call-update) | async-done | bytes 1835024 | tf_op jit(solution)/shard_map/all_gather | solution.py:45
  105.3 3.9 fusion.7
  109.2 0.0 copy-start.5
  109.2 0.0 copy-start.1
  109.2 0.0 all-gather.7.cloned.1.call-update
  109.2 0.0 all-reduce.5.cloned.1.call-start
  109.2 0.6 copy-done.5
  109.9 0.8 copy-done.1
  110.7 0.5 fusion.1
  111.2 488.3 %all-gather.7.cloned.1.call-done = f32[1792,3584]{1,0:T(8,128)} async-done(((f32[224,3584]{1,0:T(8,128)}), f32[1792,3584]{1,0:T(8,128)}) %all-gather.7.cloned.1.call-update) | async-done | bytes 25690128 | tf_op jit(solution)/shard_map/all_gather | solution.py:13
  599.5 11.5 %reduce_sum.39 = f32[224,3584]{1,0:T(8,128)} reduce(f32[8,224,3584]{2,1,0:T(8,128)} %bitcast.30, f32[]{:T(128)} %constant.6.clone.1), dimensions={0}, to_apply=%region_2.3 | reduce | flops 5619712 | bytes 28901380 | tf_op jit(solution)/shard_map/reduce_sum | solution.py:14
  611.1 2.9 fusion.3
  614.0 0.0 copy-start.2
  614.0 1.1 copy-done.2
  615.1 1.3 fusion.5
  616.4 0.0 all-reduce.5.cloned.1.call-update
  616.4 0.0 reduce-scatter.5.cloned.1.call-start
  616.5 3.4 fusion
  619.8 0.0 copy-start.4
  619.8 0.0 reduce-scatter.5.cloned.1.call-update
  619.9 2.6 psum.23
  622.5 12.2 %all-reduce.5.cloned.1.call-done = f32[224,256]{1,0:T(8,128)} async-done(((f32[224,256]{1,0:T(8,128)}), f32[224,256]{1,0:T(8,128)}) %all-reduce.5.cloned.1.call-update) | async-done | bytes 229392 | tf_op jit(solution)/shard_map/psum | solution.py:55
  634.7 0.0 copy-done.4
  634.7 1.0 multiply_convert_fusion
  635.7 6.0 all_gather.15
  641.7 2.1 fusion.4
  643.8 1.5 reduce_sum.41
  645.3 2.2 copy.10
  647.5 20.1 %reduce-scatter.5.cloned.1.call-done = bf16[1792,256]{1,0:T(8,128)(2,1)} async-done(((bf16[3584,256]{1,0:T(8,128)(2,1)}), bf16[1792,256]{1,0:T(8,128)(2,1)}) %reduce-scatter.5.cloned.1.call-update) | async-done | bytes 917520 | tf_op jit(solution)/shard_map/reduce_scatter | solution.py:63
  (4 shorter events, 0.1 us)
Async XLA Ops:
  7.2 28.7 %copy-start = (bf16[1,1792,256]{2,1,0:T(8,128)(2,1)S(1)}, bf16[1,1792,256]{2,1,0:T(8,128)(2,1)}, u32[]{:S(2)}) copy-start(bf16[1,1792,256]{2,1,0:T(8,128)(2,1)} %param.8) | copy-start | bytes 2752516
  7.2 44.7 %reduce-scatter.3.cloned.1.call-start = ((), (), s32[]{:S(2)}) async-start(), calls=%async_computation.3 | async-start | bytes 688128 | tf_op jit(solution)/shard_map/reduce_scatter | solution.py:37
  34.7 1.2 copy-start.3
  35.9 16.7 %copy-start.7 = (s32[224]{0:T(256)S(1)}, s32[224]{0:T(256)}, u32[]{:S(2)}) copy-start(s32[224]{0:T(256)} %param.7) | copy-start | bytes 2692
  35.9 36.4 %copy-start.6 = (f32[256]{0:T(256)S(1)}, f32[256]{0:T(256)}, u32[]{:S(2)}) copy-start(f32[256]{0:T(256)} %param.9) | copy-start | bytes 3076
  37.3 35.0 %all-reduce.3.cloned.1.call-start = ((), (), s32[]{:S(2)}) async-start(), calls=%async_computation.4 | async-start | bytes 458752 | tf_op jit(solution)/shard_map/psum | solution.py:43
  51.9 53.4 %all-gather.5.cloned.1.call-start = ((), (), s32[]{:S(2)}) async-start(), calls=%async_computation.7 | async-start | bytes 2752512 | tf_op jit(solution)/shard_map/all_gather | solution.py:45
  52.6 546.9 %all-gather.7.cloned.1.call-start = ((), (), s32[]{:S(2)}) async-start(), calls=%async_computation.8 | async-start | bytes 28901376 | tf_op jit(solution)/shard_map/all_gather | solution.py:13
  109.2 0.7 copy-start.5
  109.2 1.5 copy-start.1
  109.2 525.5 %all-reduce.5.cloned.1.call-start = ((), (), s32[]{:S(2)}) async-start(), calls=%async_computation.5 | async-start | bytes 458752 | tf_op jit(solution)/shard_map/psum | solution.py:55
  614.0 1.2 copy-start.2
  616.4 51.2 %reduce-scatter.5.cloned.1.call-start = ((), (), s32[]{:S(2)}) async-start(), calls=%async_computation.6 | async-start | bytes 2752512 | tf_op jit(solution)/shard_map/reduce_scatter | solution.py:63
  619.8 14.8 %copy-start.4 = (f32[224,256]{1,0:T(8,128)S(1)}, f32[224,256]{1,0:T(8,128)}, u32[]{:S(2)}) copy-start(f32[224,256]{1,0:T(8,128)} %all-reduce.3.cloned.1.call-done) | copy-start | bytes 688132
Sparse Core Ops, SparseCore 0:
  37.4 14.3 reduce-scatter.2
  54.2 18.1 all-reduce.2
  73.9 31.3 all-gather.4
  109.3 490.1 all-gather.6
  616.5 18.0 all-reduce.4
  637.3 30.2 reduce-scatter.4
